TPU v7x, 32 devices: a whole 2x2x4 slice. The times are simulated.
32 devices in a mesh: segment: 2 (over y), frame: 16 (over z, x, core).
Axes of the slice: x: 2, y: 2, z: 4, core: 2. Of those that a mesh axis runs over, the one named last changes fastest.
Arguments:
- noisy_clips: bfloat16 [4, 16, 16, 16, 512], P(None, 'frame'), may hold values from -6 to 6
- conv_first: bfloat16 [2, 9, 512, 512], P('segment', None, 'frame'), may hold values from -0.09375 to 0.09375
- conv_second: bfloat16 [2, 9, 512, 512], P('segment', None, 'frame'), may hold values from -0.09375 to 0.09375
- temporal: bfloat16 [2, 3, 512, 512], P('segment', None, 'frame'), may hold values from -0.15625 to 0.15625
Outputs:
- denoised: bfloat16 [4, 16, 16, 16, 512], P(None, 'frame', 'segment')
All inputs are finite; a program needn't handle non-finite values.
Results may differ from a plain program's by a relative error of at most 0.013.
Values may be sent and summed in bfloat16 or wider, within the bound.
A program may use at most 64 MiB of HBM per device.

v0:
```python
import jax
import jax.numpy as jnp
from jax import lax
from jax.sharding import PartitionSpec as P

skip_scale = 0.7071067811865476


def passed_along(shard, axis, by):
    length = lax.axis_size(axis)
    pairs = [(i, i + by) for i in range(length) if 0 <= i + by < length]
    return lax.ppermute(shard, axis, pairs)


def extended_2(cells, sides, width):
    for axis, dim in sides:
        count = lax.axis_size(axis)
        ends = count - 1
        head = lax.slice_in_dim(cells, 0, width, axis=dim)
        tail = lax.slice_in_dim(cells, cells.shape[dim] - width, cells.shape[dim], axis=dim)
        cells = jnp.concatenate(
            [
                lax.ppermute(tail, axis, [(i, (i + 1) % count) for i in range(ends)]),
                cells,
                lax.ppermute(head, axis, [((i + 1) % count, i) for i in range(ends)]),
            ],
            axis=dim,
        )
    return cells


def broadcast(shard, axis, root):
    mine = lax.axis_index(axis) == root
    return lax.psum(jnp.where(mine, shard, jnp.zeros_like(shard)), axis)


def spatial(field_in, kernel):
    extent = field_in.shape[1]
    channels = field_in.shape[3]
    padded = jnp.pad(field_in, ((0, 0), (1, 1), (1, 1), (0, 0)))
    accumulated = jnp.zeros((field_in.shape[0] * extent * extent, channels), jnp.float32)
    for row_shift in range(3):
        for col_shift in range(3):
            window = padded[
                :, row_shift : row_shift + extent, col_shift : col_shift + extent, :
            ].reshape(-1, channels)
            accumulated = accumulated + jnp.dot(
                window, kernel[3 * row_shift + col_shift], preferred_element_type=jnp.float32
            )
    return accumulated.reshape(field_in.shape)


def temporal_mix(extended, kernel, frame_local):
    channels = extended.shape[3]
    out_shape = (frame_local,) + extended.shape[1:]
    accumulated = jnp.zeros(out_shape, jnp.float32)
    for offset in range(3):
        window = extended[offset : offset + frame_local].reshape(-1, channels)
        accumulated = accumulated + jnp.dot(
            window, kernel[offset], preferred_element_type=jnp.float32
        ).reshape(out_shape)
    return accumulated


def on_device(noisy_clips, conv_first, conv_second, temporal):
    sections = lax.axis_size("segment")
    segment_id = lax.axis_index("segment")
    first_full, second_full, time_full = (
        lax.all_gather(conv_first, "frame", axis=2, tiled=True),
        lax.all_gather(conv_second, "frame", axis=2, tiled=True),
        lax.all_gather(temporal, "frame", axis=2, tiled=True),
    )
    first_kernel = first_full[0]
    second_kernel = second_full[0]
    time_kernel = time_full[0]
    clip_count = noisy_clips.shape[0]
    frame_local = noisy_clips.shape[1]
    side_len = noisy_clips.shape[2]
    block_shape = noisy_clips.shape[1:]
    tick_count = clip_count + sections - 1
    half_sections = sections // 2
    is_up = segment_id >= half_sections
    store_depth = max(half_sections - 1, 1)
    side_store = jnp.zeros((store_depth,) + block_shape, jnp.bfloat16)
    out_store = jnp.zeros(noisy_clips.shape, jnp.bfloat16)
    prev_out = jnp.zeros(block_shape, jnp.bfloat16)

    def tick_step(carry, tick_index):
        prev_out, side_store, out_store = carry
        clip_now = tick_index - segment_id
        active = (clip_now >= 0) & (clip_now < clip_count)
        clip_slot = jnp.clip(clip_now, 0, clip_count - 1)
        own_input = lax.dynamic_index_in_dim(noisy_clips, clip_slot, 0, keepdims=False)
        received, side_store = passed_along((prev_out, side_store), "segment", 1)
        entering = jnp.where(segment_id == 0, own_input, received)
        written = (jnp.arange(store_depth) == segment_id - 1) & (segment_id < half_sections)
        side_store = jnp.where(written[:, None, None, None, None], entering[None], side_store)
        stack_slot = jnp.clip(sections - 2 - segment_id, 0, store_depth - 1)
        stored = lax.dynamic_index_in_dim(side_store, stack_slot, 0, keepdims=False)
        skip_feature = jnp.where(segment_id == sections - 1, own_input, stored)
        joined = (
            (entering.astype(jnp.float32) + skip_feature.astype(jnp.float32)) * skip_scale
        ).astype(jnp.bfloat16)
        section_in = jnp.where(is_up, joined, entering)
        activated = lax.cond(
            active,
            lambda: jax.nn.silu(spatial(section_in, first_kernel)).astype(jnp.bfloat16),
            lambda: jnp.zeros(block_shape, jnp.bfloat16),
        )
        extended = extended_2(activated, (("frame", 0),), 1)

        def second_pass():
            branch_sum = spatial(activated, second_kernel) + temporal_mix(
                extended, time_kernel, frame_local
            )
            return (section_in.astype(jnp.float32) + jax.nn.silu(branch_sum)).astype(jnp.bfloat16)

        section_out = lax.cond(active, second_pass, lambda: jnp.zeros(block_shape, jnp.bfloat16))
        finished = (jnp.arange(clip_count) == clip_slot) & active & (segment_id == sections - 1)
        out_store = jnp.where(finished[:, None, None, None, None], section_out[None], out_store)
        return ((section_out, side_store, out_store), None)

    final_carry, unused = lax.scan(
        tick_step, (prev_out, side_store, out_store), jnp.arange(tick_count, dtype=jnp.int32)
    )
    delivered = broadcast(final_carry[2], "segment", sections - 1)
    slab_rows = side_len // sections
    return lax.dynamic_slice_in_dim(delivered, segment_id * slab_rows, slab_rows, 2)


def solution(mesh):
    in_specs = (
        P(None, "frame", None, None, None),
        P("segment", None, "frame", None),
        P("segment", None, "frame", None),
        P("segment", None, "frame", None),
    )
    out_specs = P(None, "frame", "segment", None, None)
    return jax.shard_map(
        on_device, mesh=mesh, in_specs=in_specs, out_specs=out_specs, check_vma=False
    )
```

profile of v0, /device:TPU:2, one launch (start us, length us, event | category | flops | bytes accessed | tf_op | source)
XLA Modules:
  0.0 427.1 jit_solution(14071804297938684224)
XLA Ops:
  8.8 40.6 %all-gather.8.cloned.1.call-done = bf16[1,3,512,512]{3,2,1,0:T(8,128)(2,1)} async-done(((bf16[1,3,32,512]{3,2,1,0:T(8,128)(2,1)}), bf16[1,3,512,512]{3,2,1,0:T(8,128)(2,1)}) %all-gather.8.cloned.1.call-update) | async-done | bytes 1572880 | tf_op jit(solution)/shard_map/all_gather | solution.py:71
  49.4 54.0 %all-gather.4.cloned.1.call-done = bf16[1,9,512,512]{3,2,1,0:T(8,128)(2,1)} async-done(((bf16[1,9,32,512]{3,2,1,0:T(8,128)(2,1)}), bf16[1,9,512,512]{3,2,1,0:T(8,128)(2,1)}) %all-gather.4.cloned.1.call-update) | async-done | bytes 4718608 | tf_op jit(solution)/shard_map/all_gather | solution.py:69
  103.4 53.7 %all-gather.6.cloned.1.call-done = bf16[1,9,512,512]{3,2,1,0:T(8,128)(2,1)} async-done(((bf16[1,9,32,512]{3,2,1,0:T(8,128)(2,1)}), bf16[1,9,512,512]{3,2,1,0:T(8,128)(2,1)}) %all-gather.6.cloned.1.call-update) | async-done | bytes 4718608 | tf_op jit(solution)/shard_map/all_gather | solution.py:70
  157.8 202.2 %while.17 = (s32[]{:T(128)}, bf16[1,16,16,512]{3,2,1,0:T(8,128)(2,1)}, bf16[1,1,16,16,512]{4,3,2,1,0:T(8,128)(2,1)}, bf16[4,1,16,16,512]{4,3,2,1,0:T(8,128)(2,1)...) while((s32[]{:T(128)}, ...), condition=%wide.region_5.6_spmd.clone, body=%wide.region_0.5_spmd.clone.sunk | while | flops 2824994816 | bytes 95421016 | solution.py:123
  167.9 5.0 %collective-permute-done = bf16[1,16,16,512]{3,2,1,0:T(8,128)(2,1)S(1)} collective-permute-done((bf16[1,16,16,512]{3,2,1,0:T(8,128)(2,1)}, bf16[1,16,16,512]{3,2,1,0:T(8,128)(2,1)S(1)}, u32[]{:S(2)}, u32[]{:S(2)}) %collective-permute-start) | collective-permute-done | bytes 262176 | tf_op jit(solution)/shard_map/while/body/eval_jaxpr/ppermute | solution.py:12
  174.9 5.4 %conditional.6 = (bf16[1,16,16,512]{3,2,1,0:T(8,128)(2,1)S(1)}) conditional(s32[]{:T(128)} %convert_element_type.72, () %tuple.67, (bf16[1,16,16,512]{3,2,1,0:T(8,128)(2,1)S(1)}, bf16[9,512,512]{2,1,0:T(8,128)(2,1)}) %tuple.68), branch_computations={%region_1.1_spmd, %region_2.2_spmd} | conditional | flops 1209663488 | bytes 38010916 | solution.py:105
  189.8 8.0 %conditional.7 = (bf16[1,16,16,512]{3,2,1,0:T(8,128)(2,1)}) conditional(s32[]{:T(128)} %convert_element_type.72, () %tuple.66, (bf16[1,16,16,512]{3,2,1,0:T(8,128)(2,1)S(1)}, bf16[1,16,16,512]{3,2,1,0:T(8,128)(2,1)S(1)}, bf16[9,512,512]{2,1,0:T(8,128)(2,1)}, bf16[1,16,16,512]{3,2,1,0:T(8,128)(2,1)S(1)}, bf16[3,512,512]{2,1,0:T(8,128)(2,1)S(1)}, ...), branch_computations={%region_3.3_spmd, %region_4.4_spmd} | conditional | flops 1612972032 | bytes 42729508 | solution.py:118
  205.2 5.5 %collective-permute-done = bf16[1,16,16,512]{3,2,1,0:T(8,128)(2,1)S(1)} collective-permute-done((bf16[1,16,16,512]{3,2,1,0:T(8,128)(2,1)}, bf16[1,16,16,512]{3,2,1,0:T(8,128)(2,1)S(1)}, u32[]{:S(2)}, u32[]{:S(2)}) %collective-permute-start) | collective-permute-done | bytes 262176 | tf_op jit(solution)/shard_map/while/body/eval_jaxpr/ppermute | solution.py:12
  212.7 5.4 %conditional.6 = (bf16[1,16,16,512]{3,2,1,0:T(8,128)(2,1)S(1)}) conditional(s32[]{:T(128)} %convert_element_type.72, () %tuple.67, (bf16[1,16,16,512]{3,2,1,0:T(8,128)(2,1)S(1)}, bf16[9,512,512]{2,1,0:T(8,128)(2,1)}) %tuple.68), branch_computations={%region_1.1_spmd, %region_2.2_spmd} | conditional | flops 1209663488 | bytes 38010916 | solution.py:105
  218.1 5.0 %collective-permute-start.2 = (bf16[1,16,16,512]{3,2,1,0:T(8,128)(2,1)S(1)}, bf16[1,16,16,512]{3,2,1,0:T(8,128)(2,1)S(1)}, u32[]{:S(2)}, u32[]{:S(2)}) collective-permute-start(bf16[1,16,16,512]{3,2,1,0:T(8,128)(2,1)S(1)} %get-tuple-element.419), channel_id=1, source_target_pairs={{0,1},{1,2},{2,3},{3,4},{4,5},{5,6},{6,7},{7,8},{8,9},{9,10},{10,1... | collective-permute-start | bytes 786440 | tf_op jit(solution)/shard_map/while/body/eval_jaxpr/ppermute | solution.py:23
  229.3 8.0 %conditional.7 = (bf16[1,16,16,512]{3,2,1,0:T(8,128)(2,1)}) conditional(s32[]{:T(128)} %convert_element_type.72, () %tuple.66, (bf16[1,16,16,512]{3,2,1,0:T(8,128)(2,1)S(1)}, bf16[1,16,16,512]{3,2,1,0:T(8,128)(2,1)S(1)}, bf16[9,512,512]{2,1,0:T(8,128)(2,1)}, bf16[1,16,16,512]{3,2,1,0:T(8,128)(2,1)S(1)}, bf16[3,512,512]{2,1,0:T(8,128)(2,1)S(1)}, ...), branch_computations={%region_3.3_spmd, %region_4.4_spmd} | conditional | flops 1612972032 | bytes 42729508 | solution.py:118
  239.5 4.3 %collective-permute-start.1 = (bf16[1,1,16,16,512]{4,3,2,1,0:T(8,128)(2,1)S(1)}, bf16[1,1,16,16,512]{4,3,2,1,0:T(8,128)(2,1)S(1)}, u32[]{:S(2)}, u32[]{:S(2)}) collective-permute-start(bf16[1,1,16,16,512]{4,3,2,1,0:T(8,128)(2,1)S(1)} %broadcast_select_fusion.3), channel_id=1, source_target_pairs={{0,16},{1,17},{2,18},{3,19},{4,20},{5,21},{6,22},{7,23},{8,24},{9,... | collective-permute-start | bytes 786440 | tf_op jit(solution)/shard_map/while/body/eval_jaxpr/ppermute | solution.py:12
  253.5 5.4 %conditional.6 = (bf16[1,16,16,512]{3,2,1,0:T(8,128)(2,1)S(1)}) conditional(s32[]{:T(128)} %convert_element_type.72, () %tuple.67, (bf16[1,16,16,512]{3,2,1,0:T(8,128)(2,1)S(1)}, bf16[9,512,512]{2,1,0:T(8,128)(2,1)}) %tuple.68), branch_computations={%region_1.1_spmd, %region_2.2_spmd} | conditional | flops 1209663488 | bytes 38010916 | solution.py:105
  259.0 6.7 %collective-permute-start.2 = (bf16[1,16,16,512]{3,2,1,0:T(8,128)(2,1)S(1)}, bf16[1,16,16,512]{3,2,1,0:T(8,128)(2,1)S(1)}, u32[]{:S(2)}, u32[]{:S(2)}) collective-permute-start(bf16[1,16,16,512]{3,2,1,0:T(8,128)(2,1)S(1)} %get-tuple-element.419), channel_id=1, source_target_pairs={{0,1},{1,2},{2,3},{3,4},{4,5},{5,6},{6,7},{7,8},{8,9},{9,10},{10,1... | collective-permute-start | bytes 786440 | tf_op jit(solution)/shard_map/while/body/eval_jaxpr/ppermute | solution.py:23
  267.6 6.3 %collective-permute-done.3 = bf16[1,16,16,512]{3,2,1,0:T(8,128)(2,1)} collective-permute-done((bf16[1,16,16,512]{3,2,1,0:T(8,128)(2,1)S(1)}, bf16[1,16,16,512]{3,2,1,0:T(8,128)(2,1)}, u32[]{:S(2)}, u32[]{:S(2)}) %collective-permute-start.3) | collective-permute-done | bytes 262176 | tf_op jit(solution)/shard_map/while/body/eval_jaxpr/ppermute | solution.py:25
  274.0 8.0 %conditional.7 = (bf16[1,16,16,512]{3,2,1,0:T(8,128)(2,1)}) conditional(s32[]{:T(128)} %convert_element_type.72, () %tuple.66, (bf16[1,16,16,512]{3,2,1,0:T(8,128)(2,1)S(1)}, bf16[1,16,16,512]{3,2,1,0:T(8,128)(2,1)S(1)}, bf16[9,512,512]{2,1,0:T(8,128)(2,1)}, bf16[1,16,16,512]{3,2,1,0:T(8,128)(2,1)S(1)}, bf16[3,512,512]{2,1,0:T(8,128)(2,1)S(1)}, ...), branch_computations={%region_3.3_spmd, %region_4.4_spmd} | conditional | flops 1612972032 | bytes 42729508 | solution.py:118
  298.2 5.4 %conditional.6 = (bf16[1,16,16,512]{3,2,1,0:T(8,128)(2,1)S(1)}) conditional(s32[]{:T(128)} %convert_element_type.72, () %tuple.67, (bf16[1,16,16,512]{3,2,1,0:T(8,128)(2,1)S(1)}, bf16[9,512,512]{2,1,0:T(8,128)(2,1)}) %tuple.68), branch_computations={%region_1.1_spmd, %region_2.2_spmd} | conditional | flops 1209663488 | bytes 38010916 | solution.py:105
  303.7 6.7 %collective-permute-start.2 = (bf16[1,16,16,512]{3,2,1,0:T(8,128)(2,1)S(1)}, bf16[1,16,16,512]{3,2,1,0:T(8,128)(2,1)S(1)}, u32[]{:S(2)}, u32[]{:S(2)}) collective-permute-start(bf16[1,16,16,512]{3,2,1,0:T(8,128)(2,1)S(1)} %get-tuple-element.419), channel_id=1, source_target_pairs={{0,1},{1,2},{2,3},{3,4},{4,5},{5,6},{6,7},{7,8},{8,9},{9,10},{10,1... | collective-permute-start | bytes 786440 | tf_op jit(solution)/shard_map/while/body/eval_jaxpr/ppermute | solution.py:23
  312.3 6.3 %collective-permute-done.3 = bf16[1,16,16,512]{3,2,1,0:T(8,128)(2,1)} collective-permute-done((bf16[1,16,16,512]{3,2,1,0:T(8,128)(2,1)S(1)}, bf16[1,16,16,512]{3,2,1,0:T(8,128)(2,1)}, u32[]{:S(2)}, u32[]{:S(2)}) %collective-permute-start.3) | collective-permute-done | bytes 262176 | tf_op jit(solution)/shard_map/while/body/eval_jaxpr/ppermute | solution.py:25
  318.7 8.0 %conditional.7 = (bf16[1,16,16,512]{3,2,1,0:T(8,128)(2,1)}) conditional(s32[]{:T(128)} %convert_element_type.72, () %tuple.66, (bf16[1,16,16,512]{3,2,1,0:T(8,128)(2,1)S(1)}, bf16[1,16,16,512]{3,2,1,0:T(8,128)(2,1)S(1)}, bf16[9,512,512]{2,1,0:T(8,128)(2,1)}, bf16[1,16,16,512]{3,2,1,0:T(8,128)(2,1)S(1)}, bf16[3,512,512]{2,1,0:T(8,128)(2,1)S(1)}, ...), branch_computations={%region_3.3_spmd, %region_4.4_spmd} | conditional | flops 1612972032 | bytes 42729508 | solution.py:118
  328.9 4.3 %collective-permute-start.1 = (bf16[1,1,16,16,512]{4,3,2,1,0:T(8,128)(2,1)S(1)}, bf16[1,1,16,16,512]{4,3,2,1,0:T(8,128)(2,1)S(1)}, u32[]{:S(2)}, u32[]{:S(2)}) collective-permute-start(bf16[1,1,16,16,512]{4,3,2,1,0:T(8,128)(2,1)S(1)} %broadcast_select_fusion.3), channel_id=1, source_target_pairs={{0,16},{1,17},{2,18},{3,19},{4,20},{5,21},{6,22},{7,23},{8,24},{9,... | collective-permute-start | bytes 786440 | tf_op jit(solution)/shard_map/while/body/eval_jaxpr/ppermute | solution.py:12
  343.0 6.7 %collective-permute-start.2 = (bf16[1,16,16,512]{3,2,1,0:T(8,128)(2,1)S(1)}, bf16[1,16,16,512]{3,2,1,0:T(8,128)(2,1)S(1)}, u32[]{:S(2)}, u32[]{:S(2)}) collective-permute-start(bf16[1,16,16,512]{3,2,1,0:T(8,128)(2,1)S(1)} %get-tuple-element.419), channel_id=1, source_target_pairs={{0,1},{1,2},{2,3},{3,4},{4,5},{5,6},{6,7},{7,8},{8,9},{9,10},{10,1... | collective-permute-start | bytes 786440 | tf_op jit(solution)/shard_map/while/body/eval_jaxpr/ppermute | solution.py:23
  351.6 6.3 %collective-permute-done.3 = bf16[1,16,16,512]{3,2,1,0:T(8,128)(2,1)} collective-permute-done((bf16[1,16,16,512]{3,2,1,0:T(8,128)(2,1)S(1)}, bf16[1,16,16,512]{3,2,1,0:T(8,128)(2,1)}, u32[]{:S(2)}, u32[]{:S(2)}) %collective-permute-start.3) | collective-permute-done | bytes 262176 | tf_op jit(solution)/shard_map/while/body/eval_jaxpr/ppermute | solution.py:25
  361.1 57.6 %all-reduce.4.cloned.1.call-done = bf16[4,1,16,16,512]{4,3,2,1,0:T(8,128)(2,1)} async-done(((bf16[4,1,16,16,512]{4,3,2,1,0:T(8,128)(2,1)}), bf16[4,1,16,16,512]{4,3,2,1,0:T(8,128)(2,1)}) %all-reduce.4.cloned.1.call-update) | async-done | bytes 1048592 | tf_op jit(solution)/shard_map/psum | solution.py:34
  (194 shorter events, 140.9 us)
Async XLA Ops:
  6.5 42.9 %all-gather.8.cloned.1.call-start = ((), (), s32[]{:S(2)}) async-start(), calls=%async_computation.2 | async-start | bytes 1671168 | tf_op jit(solution)/shard_map/all_gather | solution.py:71
  7.3 96.1 %all-gather.4.cloned.1.call-start = ((), (), s32[]{:S(2)}) async-start(), calls=%async_computation | async-start | bytes 5013504 | tf_op jit(solution)/shard_map/all_gather | solution.py:69
  8.0 149.1 %all-gather.6.cloned.1.call-start = ((), (), s32[]{:S(2)}) async-start(), calls=%async_computation.1 | async-start | bytes 5013504 | tf_op jit(solution)/shard_map/all_gather | solution.py:70
  8.7 410.0 %all-reduce.4.cloned.1.call-start = ((), (), s32[]{:S(2)}) async-start(), calls=%async_computation.3 | async-start | bytes 2097152 | tf_op jit(solution)/shard_map/psum | solution.py:34
  157.9 10.1 %collective-permute-start.1 = (bf16[1,1,16,16,512]{4,3,2,1,0:T(8,128)(2,1)S(1)}, bf16[1,1,16,16,512]{4,3,2,1,0:T(8,128)(2,1)S(1)}, u32[]{:S(2)}, u32[]{:S(2)}) collective-permute-start(bf16[1,1,16,16,512]{4,3,2,1,0:T(8,128)(2,1)S(1)} %broadcast_select_fusion.3), channel_id=1, source_target_pairs={{0,16},{1,17},{2,18},{3,19},{4,20},{5,21},{6,22},{7,23},{8,24},{9,... | collective-permute-start | bytes 786440 | tf_op jit(solution)/shard_map/while/body/eval_jaxpr/ppermute | solution.py:12
  161.3 11.7 %collective-permute-start = (bf16[1,16,16,512]{3,2,1,0:T(8,128)(2,1)}, bf16[1,16,16,512]{3,2,1,0:T(8,128)(2,1)S(1)}, u32[]{:S(2)}, u32[]{:S(2)}) collective-permute-start(bf16[1,16,16,512]{3,2,1,0:T(8,128)(2,1)} %get-tuple-element.384), channel_id=1, source_target_pairs={{0,16},{1,17},{2,18},{3,19},{4,20},{5,21},{6,22},{7,23},{8,24},{9,... | collective-permute-start | bytes 786440 | tf_op jit(solution)/shard_map/while/body/eval_jaxpr/ppermute | solution.py:12
  180.3 7.7 %collective-permute-start.2 = (bf16[1,16,16,512]{3,2,1,0:T(8,128)(2,1)S(1)}, bf16[1,16,16,512]{3,2,1,0:T(8,128)(2,1)S(1)}, u32[]{:S(2)}, u32[]{:S(2)}) collective-permute-start(bf16[1,16,16,512]{3,2,1,0:T(8,128)(2,1)S(1)} %get-tuple-element.419), channel_id=1, source_target_pairs={{0,1},{1,2},{2,3},{3,4},{4,5},{5,6},{6,7},{7,8},{8,9},{9,10},{10,1... | collective-permute-start | bytes 786440 | tf_op jit(solution)/shard_map/while/body/eval_jaxpr/ppermute | solution.py:23
  182.3 7.5 %collective-permute-start.3 = (bf16[1,16,16,512]{3,2,1,0:T(8,128)(2,1)S(1)}, bf16[1,16,16,512]{3,2,1,0:T(8,128)(2,1)}, u32[]{:S(2)}, u32[]{:S(2)}) collective-permute-start(bf16[1,16,16,512]{3,2,1,0:T(8,128)(2,1)S(1)} %get-tuple-element.419), channel_id=1, source_target_pairs={{1,0},{2,1},{3,2},{4,3},{5,4},{6,5},{7,6},{8,7},{9,8},{10,9},{11,1... | collective-permute-start | bytes 786440 | tf_op jit(solution)/shard_map/while/body/eval_jaxpr/ppermute | solution.py:25
  200.1 5.2 %collective-permute-start.1 = (bf16[1,1,16,16,512]{4,3,2,1,0:T(8,128)(2,1)S(1)}, bf16[1,1,16,16,512]{4,3,2,1,0:T(8,128)(2,1)S(1)}, u32[]{:S(2)}, u32[]{:S(2)}) collective-permute-start(bf16[1,1,16,16,512]{4,3,2,1,0:T(8,128)(2,1)S(1)} %broadcast_select_fusion.3), channel_id=1, source_target_pairs={{0,16},{1,17},{2,18},{3,19},{4,20},{5,21},{6,22},{7,23},{8,24},{9,... | collective-permute-start | bytes 786440 | tf_op jit(solution)/shard_map/while/body/eval_jaxpr/ppermute | solution.py:12
  201.4 9.4 %collective-permute-start = (bf16[1,16,16,512]{3,2,1,0:T(8,128)(2,1)}, bf16[1,16,16,512]{3,2,1,0:T(8,128)(2,1)S(1)}, u32[]{:S(2)}, u32[]{:S(2)}) collective-permute-start(bf16[1,16,16,512]{3,2,1,0:T(8,128)(2,1)} %get-tuple-element.384), channel_id=1, source_target_pairs={{0,16},{1,17},{2,18},{3,19},{4,20},{5,21},{6,22},{7,23},{8,24},{9,... | collective-permute-start | bytes 786440 | tf_op jit(solution)/shard_map/while/body/eval_jaxpr/ppermute | solution.py:12
  218.1 7.7 %collective-permute-start.2 = (bf16[1,16,16,512]{3,2,1,0:T(8,128)(2,1)S(1)}, bf16[1,16,16,512]{3,2,1,0:T(8,128)(2,1)S(1)}, u32[]{:S(2)}, u32[]{:S(2)}) collective-permute-start(bf16[1,16,16,512]{3,2,1,0:T(8,128)(2,1)S(1)} %get-tuple-element.419), channel_id=1, source_target_pairs={{0,1},{1,2},{2,3},{3,4},{4,5},{5,6},{6,7},{7,8},{8,9},{9,10},{10,1... | collective-permute-start | bytes 786440 | tf_op jit(solution)/shard_map/while/body/eval_jaxpr/ppermute | solution.py:23
  223.2 6.1 %collective-permute-start.3 = (bf16[1,16,16,512]{3,2,1,0:T(8,128)(2,1)S(1)}, bf16[1,16,16,512]{3,2,1,0:T(8,128)(2,1)}, u32[]{:S(2)}, u32[]{:S(2)}) collective-permute-start(bf16[1,16,16,512]{3,2,1,0:T(8,128)(2,1)S(1)} %get-tuple-element.419), channel_id=1, source_target_pairs={{1,0},{2,1},{3,2},{4,3},{5,4},{6,5},{7,6},{8,7},{9,8},{10,9},{11,1... | collective-permute-start | bytes 786440 | tf_op jit(solution)/shard_map/while/body/eval_jaxpr/ppermute | solution.py:25
  239.5 8.2 %collective-permute-start.1 = (bf16[1,1,16,16,512]{4,3,2,1,0:T(8,128)(2,1)S(1)}, bf16[1,1,16,16,512]{4,3,2,1,0:T(8,128)(2,1)S(1)}, u32[]{:S(2)}, u32[]{:S(2)}) collective-permute-start(bf16[1,1,16,16,512]{4,3,2,1,0:T(8,128)(2,1)S(1)} %broadcast_select_fusion.3), channel_id=1, source_target_pairs={{0,16},{1,17},{2,18},{3,19},{4,20},{5,21},{6,22},{7,23},{8,24},{9,... | collective-permute-start | bytes 786440 | tf_op jit(solution)/shard_map/while/body/eval_jaxpr/ppermute | solution.py:12
  243.9 7.7 %collective-permute-start = (bf16[1,16,16,512]{3,2,1,0:T(8,128)(2,1)}, bf16[1,16,16,512]{3,2,1,0:T(8,128)(2,1)S(1)}, u32[]{:S(2)}, u32[]{:S(2)}) collective-permute-start(bf16[1,16,16,512]{3,2,1,0:T(8,128)(2,1)} %get-tuple-element.384), channel_id=1, source_target_pairs={{0,16},{1,17},{2,18},{3,19},{4,20},{5,21},{6,22},{7,23},{8,24},{9,... | collective-permute-start | bytes 786440 | tf_op jit(solution)/shard_map/while/body/eval_jaxpr/ppermute | solution.py:12
  259.0 8.6 %collective-permute-start.2 = (bf16[1,16,16,512]{3,2,1,0:T(8,128)(2,1)S(1)}, bf16[1,16,16,512]{3,2,1,0:T(8,128)(2,1)S(1)}, u32[]{:S(2)}, u32[]{:S(2)}) collective-permute-start(bf16[1,16,16,512]{3,2,1,0:T(8,128)(2,1)S(1)} %get-tuple-element.419), channel_id=1, source_target_pairs={{0,1},{1,2},{2,3},{3,4},{4,5},{5,6},{6,7},{7,8},{8,9},{9,10},{10,1... | collective-permute-start | bytes 786440 | tf_op jit(solution)/shard_map/while/body/eval_jaxpr/ppermute | solution.py:23
  265.7 8.3 %collective-permute-start.3 = (bf16[1,16,16,512]{3,2,1,0:T(8,128)(2,1)S(1)}, bf16[1,16,16,512]{3,2,1,0:T(8,128)(2,1)}, u32[]{:S(2)}, u32[]{:S(2)}) collective-permute-start(bf16[1,16,16,512]{3,2,1,0:T(8,128)(2,1)S(1)} %get-tuple-element.419), channel_id=1, source_target_pairs={{1,0},{2,1},{3,2},{4,3},{5,4},{6,5},{7,6},{8,7},{9,8},{10,9},{11,1... | collective-permute-start | bytes 786440 | tf_op jit(solution)/shard_map/while/body/eval_jaxpr/ppermute | solution.py:25
  284.2 8.2 %collective-permute-start.1 = (bf16[1,1,16,16,512]{4,3,2,1,0:T(8,128)(2,1)S(1)}, bf16[1,1,16,16,512]{4,3,2,1,0:T(8,128)(2,1)S(1)}, u32[]{:S(2)}, u32[]{:S(2)}) collective-permute-start(bf16[1,1,16,16,512]{4,3,2,1,0:T(8,128)(2,1)S(1)} %broadcast_select_fusion.3), channel_id=1, source_target_pairs={{0,16},{1,17},{2,18},{3,19},{4,20},{5,21},{6,22},{7,23},{8,24},{9,... | collective-permute-start | bytes 786440 | tf_op jit(solution)/shard_map/while/body/eval_jaxpr/ppermute | solution.py:12
  288.6 7.7 %collective-permute-start = (bf16[1,16,16,512]{3,2,1,0:T(8,128)(2,1)}, bf16[1,16,16,512]{3,2,1,0:T(8,128)(2,1)S(1)}, u32[]{:S(2)}, u32[]{:S(2)}) collective-permute-start(bf16[1,16,16,512]{3,2,1,0:T(8,128)(2,1)} %get-tuple-element.384), channel_id=1, source_target_pairs={{0,16},{1,17},{2,18},{3,19},{4,20},{5,21},{6,22},{7,23},{8,24},{9,... | collective-permute-start | bytes 786440 | tf_op jit(solution)/shard_map/while/body/eval_jaxpr/ppermute | solution.py:12
  303.7 8.6 %collective-permute-start.2 = (bf16[1,16,16,512]{3,2,1,0:T(8,128)(2,1)S(1)}, bf16[1,16,16,512]{3,2,1,0:T(8,128)(2,1)S(1)}, u32[]{:S(2)}, u32[]{:S(2)}) collective-permute-start(bf16[1,16,16,512]{3,2,1,0:T(8,128)(2,1)S(1)} %get-tuple-element.419), channel_id=1, source_target_pairs={{0,1},{1,2},{2,3},{3,4},{4,5},{5,6},{6,7},{7,8},{8,9},{9,10},{10,1... | collective-permute-start | bytes 786440 | tf_op jit(solution)/shard_map/while/body/eval_jaxpr/ppermute | solution.py:23
  310.4 8.3 %collective-permute-start.3 = (bf16[1,16,16,512]{3,2,1,0:T(8,128)(2,1)S(1)}, bf16[1,16,16,512]{3,2,1,0:T(8,128)(2,1)}, u32[]{:S(2)}, u32[]{:S(2)}) collective-permute-start(bf16[1,16,16,512]{3,2,1,0:T(8,128)(2,1)S(1)} %get-tuple-element.419), channel_id=1, source_target_pairs={{1,0},{2,1},{3,2},{4,3},{5,4},{6,5},{7,6},{8,7},{9,8},{10,9},{11,1... | collective-permute-start | bytes 786440 | tf_op jit(solution)/shard_map/while/body/eval_jaxpr/ppermute | solution.py:25
  328.9 8.2 %collective-permute-start.1 = (bf16[1,1,16,16,512]{4,3,2,1,0:T(8,128)(2,1)S(1)}, bf16[1,1,16,16,512]{4,3,2,1,0:T(8,128)(2,1)S(1)}, u32[]{:S(2)}, u32[]{:S(2)}) collective-permute-start(bf16[1,1,16,16,512]{4,3,2,1,0:T(8,128)(2,1)S(1)} %broadcast_select_fusion.3), channel_id=1, source_target_pairs={{0,16},{1,17},{2,18},{3,19},{4,20},{5,21},{6,22},{7,23},{8,24},{9,... | collective-permute-start | bytes 786440 | tf_op jit(solution)/shard_map/while/body/eval_jaxpr/ppermute | solution.py:12
  333.3 7.7 %collective-permute-start = (bf16[1,16,16,512]{3,2,1,0:T(8,128)(2,1)}, bf16[1,16,16,512]{3,2,1,0:T(8,128)(2,1)S(1)}, u32[]{:S(2)}, u32[]{:S(2)}) collective-permute-start(bf16[1,16,16,512]{3,2,1,0:T(8,128)(2,1)} %get-tuple-element.384), channel_id=1, source_target_pairs={{0,16},{1,17},{2,18},{3,19},{4,20},{5,21},{6,22},{7,23},{8,24},{9,... | collective-permute-start | bytes 786440 | tf_op jit(solution)/shard_map/while/body/eval_jaxpr/ppermute | solution.py:12
  343.0 8.7 %collective-permute-start.2 = (bf16[1,16,16,512]{3,2,1,0:T(8,128)(2,1)S(1)}, bf16[1,16,16,512]{3,2,1,0:T(8,128)(2,1)S(1)}, u32[]{:S(2)}, u32[]{:S(2)}) collective-permute-start(bf16[1,16,16,512]{3,2,1,0:T(8,128)(2,1)S(1)} %get-tuple-element.419), channel_id=1, source_target_pairs={{0,1},{1,2},{2,3},{3,4},{4,5},{5,6},{6,7},{7,8},{8,9},{9,10},{10,1... | collective-permute-start | bytes 786440 | tf_op jit(solution)/shard_map/while/body/eval_jaxpr/ppermute | solution.py:23
  349.7 8.3 %collective-permute-start.3 = (bf16[1,16,16,512]{3,2,1,0:T(8,128)(2,1)S(1)}, bf16[1,16,16,512]{3,2,1,0:T(8,128)(2,1)}, u32[]{:S(2)}, u32[]{:S(2)}) collective-permute-start(bf16[1,16,16,512]{3,2,1,0:T(8,128)(2,1)S(1)} %get-tuple-element.419), channel_id=1, source_target_pairs={{1,0},{2,1},{3,2},{4,3},{5,4},{6,5},{7,6},{8,7},{9,8},{10,9},{11,1... | collective-permute-start | bytes 786440 | tf_op jit(solution)/shard_map/while/body/eval_jaxpr/ppermute | solution.py:25
  (13 other events, 122.2 us)
Sparse Core Ops, SparseCore 0:
  9.5 39.8 all-gather.7
  51.6 51.7 all-gather.3
  105.6 51.4 all-gather.5
  361.2 57.4 all-reduce.3
where the time goes:
time: 430 us; the launch traced here: 427 us
  waiting for transfers between devices  266 us (62%)
  starting transfers between devices  62.6 us (15%)
  matrix products  50 us (12%)
  other arithmetic  22 us (5%)
  between operations  13.2 us (3%)
  local copies, waits for them, and re-layouts  8.95 us (2%)
  loops' own time  4.65 us (1%)
    psum x1, waiting for transfers between devices, broadcast(): return lax.psum(jnp.where(mine, shard, jnp.zeros_like(shard)), axis)  57.6 us
    all_gather x1, waiting for transfers between devices, on_device(): lax.all_gather(conv_first, 'frame', axis=2, tiled=True)  54 us
    all_gather x1, waiting for transfers between devices, on_device(): lax.all_gather(conv_second, 'frame', axis=2, tiled=True)  53.7 us
    all_gather x1, waiting for transfers between devices, on_device(): lax.all_gather(temporal, 'frame', axis=2, tiled=True)  40.6 us
    dot_general x72, matrix products, spatial(): jnp.dot(window, kernel[3 * row_shift + col_shift], preferred_element_type...  39.3 us
    ppermute x10, waiting for transfers between devices, passed_along(): return lax.ppermute(shard, axis, pairs)  30.8 us
    ppermute x5, starting transfers between devices, extended_2(): lax.ppermute(tail, axis, [(i, (i + 1) % count) for i in range(ends)])  27 us
    ppermute x5, waiting for transfers between devices, extended_2(): lax.ppermute(head, axis, [((i + 1) % count, i) for i in range(ends)])  24.2 us
  transfers between devices with their start and end apart: 24, of which 21 were waited for; matrix products, arithmetic and copies ran while one was open for 1% of the time, Pallas kernels for 0%

commit v1 on v0

--- a/solution.py
+++ b/solution.py
@@ -1,9 +1,181 @@
+import functools
+
 import jax
 import jax.numpy as jnp
 from jax import lax
+from jax.experimental import pallas as pl
+from jax.experimental.pallas import tpu as pltpu
 from jax.sharding import PartitionSpec as P
 
 skip_scale = 0.7071067811865476
+MESH = pl.DeviceIdType.MESH
+
+
+def stream_parts(sections, taps):
+    parts = max(1, 8 // sections)
+    edges = [taps * i // parts for i in range(parts + 1)]
+    return [
+        (rel, edges[i], edges[i + 1] - edges[i]) for rel in range(sections) for i in range(parts)
+    ]
+
+
+def gather_kernel(
+    sections, frames, streams, blk_ref, w_ref, loc_sem, y_send, y_recv, r_send, r_recv, p_send, p_recv
+):
+    taps, depth = blk_ref.shape[1], blk_ref.shape[2]
+    n = frames // 2
+    seg = lax.axis_index("segment")
+    me = lax.axis_index("frame")
+    core, chip = lax.rem(me, 2), me // 2
+    other = chip * 2 + (1 - core)
+
+    def chip_at(place):
+        return jnp.where(place < n // 2, 2 * place, 2 * (n - 1 - place) + 1)
+
+    pos = jnp.where(lax.rem(chip, 2) == 0, chip // 2, n - 1 - chip // 2)
+
+    def frame_at(place):
+        return chip_at(lax.rem(place + 2 * n, n)) * 2 + core
+
+    right, left = frame_at(pos + 1), frame_at(pos - 1)
+
+    barrier = pltpu.get_barrier_semaphore()
+    for off in range(1, sections):
+        pl.semaphore_signal(
+            barrier, inc=1, device_id=(lax.rem(seg + off, sections), me), device_id_type=MESH
+        )
+    for peer in (right, left, other):
+        pl.semaphore_signal(barrier, inc=1, device_id=(seg, peer), device_id_type=MESH)
+    pl.semaphore_wait(barrier, sections + 2)
+
+    def rows(owner):
+        return pl.ds(pl.multiple_of(owner * depth, depth), depth)
+
+    def y_copy(off):
+        peer = lax.rem(seg + off, sections)
+        return pltpu.make_async_remote_copy(
+            src_ref=blk_ref.at[peer],
+            dst_ref=w_ref.at[pl.ds(seg * taps, taps), rows(me)],
+            send_sem=y_send.at[off - 1],
+            recv_sem=y_recv.at[off - 1],
+            device_id=(peer, me),
+            device_id_type=MESH,
+        )
+
+    local = pltpu.make_async_copy(
+        blk_ref.at[seg], w_ref.at[pl.ds(seg * taps, taps), rows(me)], loc_sem
+    )
+    local.start()
+    for off in range(1, sections):
+        y_copy(off).start()
+
+    def slab(q, step):
+        rel, first, count = streams[q]
+        owner = frame_at(pos - step if q % 2 == 0 else pos + step)
+        base = lax.rem(seg + sections - rel, sections) * taps + first
+        return w_ref.at[pl.ds(base, count), rows(owner)]
+
+    def ring(q, step):
+        return pltpu.make_async_remote_copy(
+            src_ref=slab(q, step),
+            dst_ref=slab(q, step),
+            send_sem=r_send.at[q, step],
+            recv_sem=r_recv.at[q, step],
+            device_id=(seg, right if q % 2 == 0 else left),
+            device_id_type=MESH,
+        )
+
+    def paired(q, step):
+        return pltpu.make_async_remote_copy(
+            src_ref=slab(q, step),
+            dst_ref=slab(q, step),
+            send_sem=p_send.at[q, step],
+            recv_sem=p_recv.at[q, step],
+            device_id=(seg, other),
+            device_id_type=MESH,
+        )
+
+    per = len(streams) // sections
+    for rel in range(sections):
+        if rel == 0:
+            local.wait()
+        else:
+            y_copy(rel).wait_recv()
+        for q in range(rel * per, (rel + 1) * per):
+            ring(q, 0).start()
+            paired(q, 0).start()
+
+    @pl.loop(0, n - 2)
+    def _(step):
+        for q in range(len(streams)):
+            ring(q, step).wait_recv()
+            ring(q, step + 1).start()
+            paired(q, step + 1).start()
+
+    for q in range(len(streams)):
+        ring(q, n - 2).wait_recv()
+        paired(q, n - 1).start()
+
+    for off in range(1, sections):
+        y_copy(off).wait_send()
+
+    @pl.loop(0, n - 1)
+    def _(step):
+        for q in range(len(streams)):
+            ring(q, step).wait_send()
+            paired(q, step).wait()
+
+    for q in range(len(streams)):
+        paired(q, n - 1).wait()
+
+
+def gathered(blocks, sections, frames):
+    taps, depth, width = blocks.shape[1:]
+    streams = stream_parts(sections, taps)
+    count, n = len(streams), frames // 2
+    dma = pltpu.SemaphoreType.DMA
+    return pl.pallas_call(
+        functools.partial(gather_kernel, sections, frames, streams),
+        out_shape=jax.ShapeDtypeStruct((sections * taps, frames * depth, width), blocks.dtype),
+        in_specs=[pl.BlockSpec(memory_space=pltpu.VMEM)],
+        out_specs=pl.BlockSpec(memory_space=pltpu.VMEM),
+        scratch_shapes=[
+            dma,
+            dma((max(sections - 1, 1),)),
+            dma((max(sections - 1, 1),)),
+            dma((count, n)),
+            dma((count, n)),
+            dma((count, n)),
+            dma((count, n)),
+        ],
+        compiler_params=pltpu.CompilerParams(
+            collective_id=0, has_side_effects=True, vmem_limit_bytes=58 * 1024 * 1024
+        ),
+    )(blocks)
+
+
+def conv(field, kernel):
+    lead = field.shape[:-3]
+    out = lax.conv_general_dilated(
+        field.reshape((-1,) + field.shape[-3:]),
+        kernel.reshape((3, 3) + kernel.shape[1:]),
+        (1, 1),
+        "SAME",
+        dimension_numbers=("NHWC", "HWIO", "NHWC"),
+        preferred_element_type=jnp.float32,
+    )
+    return out.reshape(lead + out.shape[1:])
+
+
+def whole_channels(piece, sections, seg):
+    if sections == 2:
+        theirs = lax.ppermute(piece, "segment", [(0, 1), (1, 0)])
+        return jnp.where(
+            seg == 0,
+            jnp.concatenate([piece, theirs], axis=-1),
+            jnp.concatenate([theirs, piece], axis=-1),
+        )
+    return lax.all_gather(piece, "segment", axis=piece.ndim - 1, tiled=True)
 
 
 def passed_along(shard, axis, by):
@@ -62,7 +234,7 @@
     return accumulated
 
 
-def on_device(noisy_clips, conv_first, conv_second, temporal):
+def pipelined(noisy_clips, conv_first, conv_second, temporal):
     sections = lax.axis_size("segment")
     segment_id = lax.axis_index("segment")
     first_full, second_full, time_full = (
@@ -128,6 +300,66 @@
     return lax.dynamic_slice_in_dim(delivered, segment_id * slab_rows, slab_rows, 2)
 
 
+def on_device(noisy_clips, conv_first, conv_second, temporal):
+    sections = lax.axis_size("segment")
+    frames = lax.axis_size("frame")
+    seg = lax.axis_index("segment")
+    channels = noisy_clips.shape[-1]
+    width = channels // sections
+    if width % 128 or frames % 4:
+        return pipelined(noisy_clips, conv_first, conv_second, temporal)
+    stacked = jnp.concatenate([conv_first[0], temporal[0], conv_second[0]], axis=0)
+    taps, depth = stacked.shape[0], stacked.shape[1]
+    blocks = stacked.reshape(taps, depth, sections, width).transpose(2, 0, 1, 3)
+    weights = gathered(blocks, sections, frames)
+    forward = [(i, i + 1) for i in range(frames - 1)]
+    backward = [(i + 1, i) for i in range(frames - 1)]
+
+    def mine(full):
+        return lax.dynamic_slice_in_dim(full, seg * width, width, full.ndim - 1)
+
+    entering = noisy_clips
+    entering_mine = mine(noisy_clips)
+    down = []
+    for s in range(sections):
+        part = weights[s * taps : (s + 1) * taps]
+        if s < sections // 2:
+            down.append(entering_mine)
+        active = jax.nn.silu(conv(entering, part[:9])).astype(jnp.bfloat16)
+        active = whole_channels(active, sections, seg)
+
+        def mixed(k):
+            return jnp.dot(active, part[9 + k], preferred_element_type=jnp.float32)
+
+        after = mixed(0).astype(jnp.bfloat16)
+        before = mixed(2).astype(jnp.bfloat16)
+        from_prev = lax.ppermute(after[:, -1:], "frame", forward)
+        from_next = lax.ppermute(before[:, :1], "frame", backward)
+        branch = conv(active, part[12:]) + mixed(1)
+        branch = branch + jnp.concatenate([from_prev, after[:, :-1]], axis=1).astype(jnp.float32)
+        branch = branch + jnp.concatenate([before[:, 1:], from_next], axis=1).astype(jnp.float32)
+        out_mine = (entering_mine.astype(jnp.float32) + jax.nn.silu(branch)).astype(jnp.bfloat16)
+        if s + 1 < sections:
+            entering_mine = out_mine
+            if s + 1 >= sections // 2:
+                skip = down[sections - 2 - s]
+                entering_mine = (
+                    (out_mine.astype(jnp.float32) + skip.astype(jnp.float32)) * skip_scale
+                ).astype(jnp.bfloat16)
+            entering = whole_channels(entering_mine, sections, seg)
+    slab = out_mine.shape[2] // sections
+    if sections == 2:
+        own = lax.dynamic_slice_in_dim(out_mine, seg * slab, slab, 2)
+        away = lax.dynamic_slice_in_dim(out_mine, (1 - seg) * slab, slab, 2)
+        theirs = lax.ppermute(away, "segment", [(0, 1), (1, 0)])
+        return jnp.where(
+            seg == 0,
+            jnp.concatenate([own, theirs], axis=-1),
+            jnp.concatenate([theirs, own], axis=-1),
+        )
+    return lax.all_to_all(out_mine, "segment", 2, 4, tiled=True)
+
+
 def solution(mesh):
     in_specs = (
         P(None, "frame", None, None, None),

time: 430 us -> 192 us (0.45)
  waiting for transfers between devices: 266 us -> 51.7 us
  Pallas kernels: 0 us -> 70 us
  starting transfers between devices: 62.6 us -> 12 us
  other arithmetic: 22 us -> 5.23 us
  matrix products: 50 us -> 33.5 us
  between operations: 13.2 us -> 0.44 us
  local copies, waits for them, and re-layouts: 8.95 us -> 18.2 us
  loops' own time: 4.65 us -> 0 us
    all_gather x3 -> x0, waiting for transfers between devices: 148 us -> none  [the longest x1 54 us: on_device(): lax.all_gather(conv_first, 'frame', axis=2, tiled=True)]
    pallas_call x0 -> x1, Pallas kernels: none -> 70 us  [gathered(): pl.pallas_call(functools.partial(gather_kernel, sections, frames, streams...]
    psum x1 -> x0, waiting for transfers between devices: 57.6 us -> none  [broadcast(): return lax.psum(jnp.where(mine, shard, jnp.zeros_like(shard)), axis)]
    ppermute x20 -> x8, starting transfers between devices: 62.5 us -> 12 us  [the longest x2 5.67 us: on_device(): from_next = lax.ppermute(before[:, :1], 'frame', backward)]
    dot_general x84 -> x6, matrix products: 50 us -> 11.1 us  [mixed(): return jnp.dot(active, part[9 + k], preferred_element_type=jnp.float32)]
    conv_general_dilated x0 -> x4, matrix products: none -> 22.4 us  [conv(): lax.conv_general_dilated(field.reshape((-1,) + field.shape[-3:]), kernel....]
    select_n x11 -> x4, other arithmetic: 17.4 us -> 3.07 us  [the longest x3 2.13 us: whole_channels(): jnp.where(seg == 0, jnp.concatenate([piece, theirs], axis=-1), jnp.concat...]
    ppermute x20 -> x8, waiting for transfers between devices: 57.8 us -> 51.7 us  [the longest x3 37.3 us: whole_channels(): theirs = lax.ppermute(piece, 'segment', [(0, 1), (1, 0)])]
  transfers between devices with their start and end apart: 24 -> 8, of which waited for: 21 -> 6; matrix products, arithmetic and copies ran while one was open for 1% -> 8% of each run, Pallas kernels for 0% -> 0%
where the time goes in v1:
time: 192 us; the launch traced here: 191 us
  Pallas kernels  70 us (36%)
  waiting for transfers between devices  51.7 us (27%)
  matrix products  33.5 us (17%)
  local copies, waits for them, and re-layouts  18.2 us (9%)
  starting transfers between devices  12 us (6%)
  other arithmetic  5.23 us (3%)
    pallas_call x1, Pallas kernels, gathered(): pl.pallas_call(functools.partial(gather_kernel, sections, frames, streams...  70 us
    ppermute x3, waiting for transfers between devices, whole_channels(): theirs = lax.ppermute(piece, 'segment', [(0, 1), (1, 0)])  37.3 us
    conv_general_dilated x4, matrix products, conv(): lax.conv_general_dilated(field.reshape((-1,) + field.shape[-3:]), kernel....  22.4 us
    dot_general x6, matrix products, mixed(): return jnp.dot(active, part[9 + k], preferred_element_type=jnp.float32)  11.1 us
    ppermute x2, waiting for transfers between devices, on_device(): from_prev = lax.ppermute(after[:, -1:], 'frame', forward)  8.59 us
    ppermute x1, waiting for transfers between devices, on_device(): theirs = lax.ppermute(away, 'segment', [(0, 1), (1, 0)])  5.85 us
    ppermute x2, starting transfers between devices, on_device(): from_next = lax.ppermute(before[:, :1], 'frame', backward)  5.67 us
    slice x1, local copies, waits for them, and re-layouts, on_device(): active = jax.nn.silu(conv(entering, part[:9])).astype(jnp.bfloat16)  5.64 us
  transfers between devices with their start and end apart: 8, of which 6 were waited for; matrix products, arithmetic and copies ran while one was open for 8% of the time, Pallas kernels for 0%

profile of v1, /device:TPU:2, one launch (start us, length us, event | category | flops | bytes accessed | tf_op | source)
XLA Modules:
  0.0 191.1 jit_solution(12104125796369624406)
XLA Ops:
  5.3 70.0 %shard_map.46 = bf16[42,512,256]{2,1,0:T(8,128)(2,1)} custom-call(bf16[2,21,32,256]{3,2,1,0:T(8,128)(2,1)} %maximum_bitcast_fusion.blk_ref), custom_call_target="tpu_custom_call" | custom-call | tf_op jit(solution)/shard_map/pallas_call | solution.py:137
  75.3 5.6 %fusion.59 = (bf16[9,512,256]{2,1,0:T(8,128)(2,1)S(1)}, bf16[9,512,256]{2,1,0:T(8,128)(2,1)S(1)}, bf16[9,512,256]{2,1,0:T(8,128)(2,1)}, bf16[9,512,256]{2,1,0:T(8,128)(2,1)}) fusion(bf16[42,512,256]{2,1,0:T(8,128)(2,1)} %shard_map.46), kind=kLoop, calls=%fused_computation.77 | loop fusion | bytes 18874368 | tf_op jit(solution)/shard_map/slice | solution.py:328
  81.0 5.6 %multiply_convert_fusion.1 = bf16[16,32,3,256]{3,1,2,0:T(8,128)(2,1)S(1)} fusion(bf16[3,3,512,256]{3,2,1,0:T(8,128)(2,1)S(1)} %bitcast.170, bf16[16,4,8,5,512]{4,0,3,2,1:T(8,128)(2,1)S(1)} %fusion.4, pred[32,3]{0,1:T(4,128)(4,1)S(1)} %copy-done.6), kind=kOutput, calls=%fused_computation.22 | convolution fusion | flops 3475243008 | bytes 5767264 | tf_op jit(solution)/shard_map/conv_general_dilated | solution.py:159
  87.8 13.7 %collective-permute-done = bf16[4,1,16,16,256]{4,3,2,0,1:T(8,128)(2,1)S(1)} collective-permute-done((bf16[4,1,16,16,256]{4,3,2,0,1:T(8,128)(2,1)S(1)}, bf16[4,1,16,16,256]{4,3,2,0,1:T(8,128)(2,1)S(1)}, u32[]{:S(2)}, u32[]{:S(2)}) %collective-permute-start) | collective-permute-done | bytes 524320 | tf_op jit(solution)/shard_map/ppermute | solution.py:172
  101.5 1.6 fusion.36
  103.0 1.4 fusion.37
  104.8 2.6 %collective-permute-start.2 = (bf16[4,1,16,16,256]{4,3,2,0,1:T(8,128)(2,1)S(1)}, bf16[4,1,16,16,256]{4,3,2,0,1:T(8,128)(2,1)S(1)}, u32[]{:S(2)}, u32[]{:S(2)}) collective-permute-start(bf16[4,1,16,16,256]{4,3,2,0,1:T(8,128)(2,1)S(1)} %fusion.37), channel_id=1, source_target_pairs={{1,0},{2,1},{3,2},{4,3},{5,4},{6,5},{7,6},{8,7},{9,8},{10,9},{11,1... | collective-permute-start | bytes 1572872 | tf_op jit(solution)/shard_map/ppermute | solution.py:337
  107.4 2.1 %collective-permute-start.1 = (bf16[4,1,16,16,256]{4,3,2,0,1:T(8,128)(2,1)S(1)}, bf16[4,1,16,16,256]{4,3,2,0,1:T(8,128)(2,1)S(1)}, u32[]{:S(2)}, u32[]{:S(2)}) collective-permute-start(bf16[4,1,16,16,256]{4,3,2,0,1:T(8,128)(2,1)S(1)} %fusion.36), channel_id=1, source_target_pairs={{0,1},{1,2},{2,3},{3,4},{4,5},{5,6},{6,7},{7,8},{8,9},{9,10},{10,1... | collective-permute-start | bytes 1572872 | tf_op jit(solution)/shard_map/ppermute | solution.py:336
  110.7 1.3 copy-done.1
  112.0 5.5 %fusion.22 = f32[16,32,3,256]{3,1,2,0:T(8,128)S(1)} fusion(bf16[3,3,512,256]{3,2,1,0:T(8,128)(2,1)S(1)} %bitcast.169, bf16[16,4,8,5,512]{4,0,3,2,1:T(8,128)(2,1)S(1)} %fusion.5, pred[32,3]{0,1:T(4,128)(4,1)S(1)} %copy-done.6), kind=kOutput, calls=%fused_computation.23 | convolution fusion | flops 3473276928 | bytes 6553696 | tf_op jit(solution)/shard_map/conv_general_dilated | solution.py:159
  118.6 3.5 %collective-permute-done.1 = bf16[4,1,16,16,256]{4,3,2,0,1:T(8,128)(2,1)S(1)} collective-permute-done((bf16[4,1,16,16,256]{4,3,2,0,1:T(8,128)(2,1)S(1)}, bf16[4,1,16,16,256]{4,3,2,0,1:T(8,128)(2,1)S(1)}, u32[]{:S(2)}, u32[]{:S(2)}) %collective-permute-start.1) | collective-permute-done | bytes 524320 | tf_op jit(solution)/shard_map/ppermute | solution.py:336
  122.1 2.2 %fusion.42 = bf16[4,1,16,16,256]{4,3,2,0,1:T(8,128)(2,1)S(1)} fusion(f32[16,4,16,256]{3,0,2,1:T(8,128)S(1)} %slice.63, bf16[4,1,16,16,256]{4,3,2,0,1:T(8,128)(2,1)S(1)} %collective-permute-done.2, bf16[4,1,16,16,256]{4,3,2,0,1:T(8,128)(2,1)S(1)} %collective-permute-done.1, bf16[4,1,16,16,512]{4,3,2,0,1:T(8,128)(2,1)S(1)} %bitcast.183, s32[]{:T(128)S(6)} %select_n.57, ...), kind=kOutput, calls=%fused_computation.45 | convolution fusion | flops 277348352 | bytes 4456453 | tf_op jit(solution)/shard_map/dot_general | solution.py:332
  124.8 12.2 %collective-permute-done.3 = bf16[4,1,16,16,256]{4,3,2,0,1:T(8,128)(2,1)S(1)} collective-permute-done((bf16[4,1,16,16,256]{4,3,2,0,1:T(8,128)(2,1)S(1)}, bf16[4,1,16,16,256]{4,3,2,0,1:T(8,128)(2,1)S(1)}, u32[]{:S(2)}, u32[]{:S(2)}) %collective-permute-start.3) | collective-permute-done | bytes 524320 | tf_op jit(solution)/shard_map/ppermute | solution.py:172
  139.9 5.8 %multiply_convert_fusion = bf16[16,32,3,256]{3,1,2,0:T(8,128)(2,1)S(1)} fusion(bf16[3,3,512,256]{3,2,1,0:T(8,128)(2,1)S(1)} %bitcast.168, bf16[16,4,8,5,512]{4,0,3,2,1:T(8,128)(2,1)S(1)} %fusion.6, pred[32,3]{0,1:T(4,128)(4,1)S(1)} %copy-done.6), kind=kOutput, calls=%fused_computation.21 | convolution fusion | flops 3475243008 | bytes 5767264 | tf_op jit(solution)/shard_map/conv_general_dilated | solution.py:159
  146.9 11.4 %collective-permute-done.4 = bf16[4,1,16,16,256]{4,3,2,0,1:T(8,128)(2,1)} collective-permute-done((bf16[4,1,16,16,256]{4,3,2,0,1:T(8,128)(2,1)S(1)}, bf16[4,1,16,16,256]{4,3,2,0,1:T(8,128)(2,1)}, u32[]{:S(2)}, u32[]{:S(2)}) %collective-permute-start.4) | collective-permute-done | bytes 524320 | tf_op jit(solution)/shard_map/ppermute | solution.py:172
  158.4 1.7 fusion.38
  160.1 1.7 fusion.39
  161.8 1.5 fusion.57
  163.3 3.1 %collective-permute-start.6 = (bf16[4,1,16,16,256]{4,3,2,0,1:T(8,128)(2,1)S(1)}, bf16[4,1,16,16,256]{4,3,2,0,1:T(8,128)(2,1)S(1)}, u32[]{:S(2)}, u32[]{:S(2)}) collective-permute-start(bf16[4,1,16,16,256]{4,3,2,0,1:T(8,128)(2,1)S(1)} %fusion.39), channel_id=1, source_target_pairs={{1,0},{2,1},{3,2},{4,3},{5,4},{6,5},{7,6},{8,7},{9,8},{10,9},{11,1... | collective-permute-start | bytes 1572872 | tf_op jit(solution)/shard_map/ppermute | solution.py:337
  166.4 1.9 %collective-permute-start.5 = (bf16[4,1,16,16,256]{4,3,2,0,1:T(8,128)(2,1)S(1)}, bf16[4,1,16,16,256]{4,3,2,0,1:T(8,128)(2,1)S(1)}, u32[]{:S(2)}, u32[]{:S(2)}) collective-permute-start(bf16[4,1,16,16,256]{4,3,2,0,1:T(8,128)(2,1)S(1)} %fusion.38), channel_id=1, source_target_pairs={{0,1},{1,2},{2,3},{3,4},{4,5},{5,6},{6,7},{7,8},{8,9},{9,10},{10,1... | collective-permute-start | bytes 1572872 | tf_op jit(solution)/shard_map/ppermute | solution.py:336
  169.5 5.5 %fusion.27 = f32[16,32,3,256]{3,1,2,0:T(8,128)S(1)} fusion(bf16[3,3,512,256]{3,2,1,0:T(8,128)(2,1)S(1)} %bitcast.167, bf16[16,4,8,5,512]{4,0,3,2,1:T(8,128)(2,1)S(1)} %fusion.7, pred[32,3]{0,1:T(4,128)(4,1)S(1)} %copy-done.6), kind=kOutput, calls=%fused_computation.24 | convolution fusion | flops 3473276928 | bytes 6553696 | tf_op jit(solution)/shard_map/conv_general_dilated | solution.py:159
  176.1 5.1 %collective-permute-done.5 = bf16[4,1,16,16,256]{4,3,2,0,1:T(8,128)(2,1)S(1)} collective-permute-done((bf16[4,1,16,16,256]{4,3,2,0,1:T(8,128)(2,1)S(1)}, bf16[4,1,16,16,256]{4,3,2,0,1:T(8,128)(2,1)S(1)}, u32[]{:S(2)}, u32[]{:S(2)}) %collective-permute-start.5) | collective-permute-done | bytes 524320 | tf_op jit(solution)/shard_map/ppermute | solution.py:336
  181.2 2.5 %add_convert_fusion = bf16[4,1,16,16,256]{4,3,2,0,1:T(8,128)(2,1)S(1)} fusion(f32[16,4,16,256]{3,0,2,1:T(8,128)S(1)} %slice.67, bf16[4,1,16,16,256]{4,3,2,0,1:T(8,128)(2,1)S(1)} %collective-permute-done.6, bf16[4,1,16,16,256]{4,3,2,0,1:T(8,128)(2,1)S(1)} %collective-permute-done.5, bf16[4,1,16,16,256]{4,3,2,0,1:T(8,128)(2,1)S(1)} %fusion.42, ...), kind=kOutput, calls=%fused_computation.53 | convolution fusion | flops 276299776 | bytes 4456449 | tf_op jit(solution)/shard_map/dot_general | solution.py:332
  184.3 5.8 %collective-permute-done.7 = bf16[4,1,8,16,256]{4,3,2,0,1:T(8,128)(2,1)S(1)} collective-permute-done((bf16[4,1,8,16,256]{4,3,2,0,1:T(8,128)(2,1)S(1)}, bf16[4,1,8,16,256]{4,3,2,0,1:T(8,128)(2,1)S(1)}, u32[]{:S(2)}, u32[]{:S(2)}) %collective-permute-start.7) | collective-permute-done | bytes 262176 | tf_op jit(solution)/shard_map/ppermute | solution.py:354
  (56 shorter events, 17.2 us)
Async XLA Ops:
  0.0 3.2 %copy-start.2 = (bf16[4,1,16,16,512]{4,3,2,1,0:T(8,128)(2,1)S(1)}, bf16[4,1,16,16,512]{4,3,2,1,0:T(8,128)(2,1)}, u32[]{:S(2)}) copy-start(bf16[4,1,16,16,512]{4,3,2,1,0:T(8,128)(2,1)} %param.4) | copy-start | bytes 3145732
  75.3 5.7 %copy-start.6 = (pred[32,3]{0,1:T(4,128)(4,1)S(1)}, pred[32,3]{0,1:T(4,128)(4,1)}, u32[]{:S(2)}) copy-start(pred[32,3]{0,1:T(4,128)(4,1)} %constant.46) | copy-start | bytes 292
  87.2 14.2 %collective-permute-start = (bf16[4,1,16,16,256]{4,3,2,0,1:T(8,128)(2,1)S(1)}, bf16[4,1,16,16,256]{4,3,2,0,1:T(8,128)(2,1)S(1)}, u32[]{:S(2)}, u32[]{:S(2)}) collective-permute-start(bf16[4,1,16,16,256]{4,3,2,0,1:T(8,128)(2,1)S(1)} %bitcast.178), channel_id=1, source_target_pairs={{0,16},{16,0},{1,17},{17,1},{2,18},{18,2},{3,19},{19,3},{4,20},{20... | collective-permute-start | bytes 1572872 | tf_op jit(solution)/shard_map/ppermute | solution.py:172
  101.5 3.0 %copy-start.4 = (bf16[4,1,16,16,256]{4,3,2,0,1:T(8,128)(2,1)}, bf16[4,1,16,16,256]{4,3,2,0,1:T(8,128)(2,1)S(1)}, u32[]{:S(2)}) copy-start(bf16[4,1,16,16,256]{4,3,2,0,1:T(8,128)(2,1)S(1)} %collective-permute-done) | copy-start | bytes 1572868
  104.8 13.8 %collective-permute-start.2 = (bf16[4,1,16,16,256]{4,3,2,0,1:T(8,128)(2,1)S(1)}, bf16[4,1,16,16,256]{4,3,2,0,1:T(8,128)(2,1)S(1)}, u32[]{:S(2)}, u32[]{:S(2)}) collective-permute-start(bf16[4,1,16,16,256]{4,3,2,0,1:T(8,128)(2,1)S(1)} %fusion.37), channel_id=1, source_target_pairs={{1,0},{2,1},{3,2},{4,3},{5,4},{6,5},{7,6},{8,7},{9,8},{10,9},{11,1... | collective-permute-start | bytes 1572872 | tf_op jit(solution)/shard_map/ppermute | solution.py:337
  107.4 14.7 %collective-permute-start.1 = (bf16[4,1,16,16,256]{4,3,2,0,1:T(8,128)(2,1)S(1)}, bf16[4,1,16,16,256]{4,3,2,0,1:T(8,128)(2,1)S(1)}, u32[]{:S(2)}, u32[]{:S(2)}) collective-permute-start(bf16[4,1,16,16,256]{4,3,2,0,1:T(8,128)(2,1)S(1)} %fusion.36), channel_id=1, source_target_pairs={{0,1},{1,2},{2,3},{3,4},{4,5},{5,6},{6,7},{7,8},{8,9},{9,10},{10,1... | collective-permute-start | bytes 1572872 | tf_op jit(solution)/shard_map/ppermute | solution.py:336
  110.3 1.7 copy-start.1
  117.5 4.5 %copy-start.3 = (bf16[4,1,16,16,512]{4,3,2,1,0:T(8,128)(2,1)S(1)}, bf16[4,1,16,16,512]{4,3,2,1,0:T(8,128)(2,1)}, u32[]{:S(2)}) copy-start(bf16[4,1,16,16,512]{4,3,2,1,0:T(8,128)(2,1)} %param.4) | copy-start | bytes 3145732
  117.5 4.5 %copy-start.5 = (bf16[4,1,16,16,256]{4,3,2,0,1:T(8,128)(2,1)S(1)}, bf16[4,1,16,16,256]{4,3,2,0,1:T(8,128)(2,1)}, u32[]{:S(2)}) copy-start(bf16[4,1,16,16,256]{4,3,2,0,1:T(8,128)(2,1)} %copy-done.4) | copy-start | bytes 1572868
  124.3 12.8 %collective-permute-start.3 = (bf16[4,1,16,16,256]{4,3,2,0,1:T(8,128)(2,1)S(1)}, bf16[4,1,16,16,256]{4,3,2,0,1:T(8,128)(2,1)S(1)}, u32[]{:S(2)}, u32[]{:S(2)}) collective-permute-start(bf16[4,1,16,16,256]{4,3,2,0,1:T(8,128)(2,1)S(1)} %fusion.42), channel_id=1, source_target_pairs={{0,16},{16,0},{1,17},{17,1},{2,18},{18,2},{3,19},{19,3},{4,20},{20... | collective-permute-start | bytes 1572872 | tf_op jit(solution)/shard_map/ppermute | solution.py:172
  138.2 1.7 copy-start
  146.4 12.0 %collective-permute-start.4 = (bf16[4,1,16,16,256]{4,3,2,0,1:T(8,128)(2,1)S(1)}, bf16[4,1,16,16,256]{4,3,2,0,1:T(8,128)(2,1)}, u32[]{:S(2)}, u32[]{:S(2)}) collective-permute-start(bf16[4,1,16,16,256]{4,3,2,0,1:T(8,128)(2,1)S(1)} %bitcast.173), channel_id=1, source_target_pairs={{0,16},{16,0},{1,17},{17,1},{2,18},{18,2},{3,19},{19,3},{4,20},{20... | collective-permute-start | bytes 1572872 | tf_op jit(solution)/shard_map/ppermute | solution.py:172
  163.3 12.7 %collective-permute-start.6 = (bf16[4,1,16,16,256]{4,3,2,0,1:T(8,128)(2,1)S(1)}, bf16[4,1,16,16,256]{4,3,2,0,1:T(8,128)(2,1)S(1)}, u32[]{:S(2)}, u32[]{:S(2)}) collective-permute-start(bf16[4,1,16,16,256]{4,3,2,0,1:T(8,128)(2,1)S(1)} %fusion.39), channel_id=1, source_target_pairs={{1,0},{2,1},{3,2},{4,3},{5,4},{6,5},{7,6},{8,7},{9,8},{10,9},{11,1... | collective-permute-start | bytes 1572872 | tf_op jit(solution)/shard_map/ppermute | solution.py:337
  166.4 14.7 %collective-permute-start.5 = (bf16[4,1,16,16,256]{4,3,2,0,1:T(8,128)(2,1)S(1)}, bf16[4,1,16,16,256]{4,3,2,0,1:T(8,128)(2,1)S(1)}, u32[]{:S(2)}, u32[]{:S(2)}) collective-permute-start(bf16[4,1,16,16,256]{4,3,2,0,1:T(8,128)(2,1)S(1)} %fusion.38), channel_id=1, source_target_pairs={{0,1},{1,2},{2,3},{3,4},{4,5},{5,6},{6,7},{7,8},{8,9},{9,10},{10,1... | collective-permute-start | bytes 1572872 | tf_op jit(solution)/shard_map/ppermute | solution.py:336
  183.7 6.4 %collective-permute-start.7 = (bf16[4,1,8,16,256]{4,3,2,0,1:T(8,128)(2,1)S(1)}, bf16[4,1,8,16,256]{4,3,2,0,1:T(8,128)(2,1)S(1)}, u32[]{:S(2)}, u32[]{:S(2)}) collective-permute-start(bf16[4,1,8,16,256]{4,3,2,0,1:T(8,128)(2,1)S(1)} %get-tuple-element.10), channel_id=1, source_target_pairs={{0,16},{16,0},{1,17},{17,1},{2,18},{18,2},{3,19},{19,3},{4,20},{20... | collective-permute-start | bytes 786440 | tf_op jit(solution)/shard_map/ppermute | solution.py:354

commit v2 on v0

--- a/solution.py
+++ b/solution.py
@@ -1,9 +1,14 @@
+import functools
+
 import jax
 import jax.numpy as jnp
 from jax import lax
+from jax.experimental import pallas as pl
+from jax.experimental.pallas import tpu as pltpu
 from jax.sharding import PartitionSpec as P
 
 skip_scale = 0.7071067811865476
+MESH = pl.DeviceIdType.MESH
 
 
 def passed_along(shard, axis, by):
@@ -62,7 +67,7 @@
     return accumulated
 
 
-def on_device(noisy_clips, conv_first, conv_second, temporal):
+def pipelined(noisy_clips, conv_first, conv_second, temporal):
     sections = lax.axis_size("segment")
     segment_id = lax.axis_index("segment")
     first_full, second_full, time_full = (
@@ -128,6 +133,401 @@
     return lax.dynamic_slice_in_dim(delivered, segment_id * slab_rows, slab_rows, 2)
 
 
+def fused_kernel(
+    frames,
+    noisy_ref,
+    first_ref,
+    second_ref,
+    time_ref,
+    out_ref,
+    w_ref,
+    xe,
+    xa,
+    a_send,
+    a_recv,
+    t_send,
+    t_recv,
+    e_mine,
+    e_recv,
+    acc_ref,
+    o_full,
+    o_take,
+    local_sem,
+    y_sems,
+    ring_sems,
+    pair_sems,
+    a_sems,
+    t_sems,
+    e_sems,
+    o_sems,
+):
+    clips, side, lanes = noisy_ref.shape[0], noisy_ref.shape[2], noisy_ref.shape[4]
+    half = lanes // 2
+    cells = side * side
+    depth = first_ref.shape[2]
+    taps = first_ref.shape[1] + time_ref.shape[1] + second_ref.shape[1]
+    n = frames // 2
+    seg = lax.axis_index("segment")
+    me = lax.axis_index("frame")
+    core, chip = lax.rem(me, 2), me // 2
+    peer = 1 - seg
+    other = chip * 2 + (1 - core)
+
+    def frame_at(place):
+        place = lax.rem(place + 2 * n, n)
+        return jnp.where(place < n // 2, 2 * place, 2 * (n - 1 - place) + 1) * 2 + core
+
+    pos = jnp.where(lax.rem(chip, 2) == 0, chip // 2, n - 1 - chip // 2)
+    right, left = frame_at(pos + 1), frame_at(pos - 1)
+    after, before = lax.rem(me + 1, frames), lax.rem(me + frames - 1, frames)
+
+    barrier = pltpu.get_barrier_semaphore()
+    pl.semaphore_signal(barrier, inc=1, device_id=(peer, me), device_id_type=MESH)
+    for target in (right, left, other, after, before):
+        pl.semaphore_signal(barrier, inc=1, device_id=(seg, target), device_id_type=MESH)
+    pl.semaphore_wait(barrier, 6)
+
+    def columns(which):
+        return pl.ds(pl.multiple_of(which * half, half), half)
+
+    parts = ((first_ref, 0, 9), (time_ref, 9, 3), (second_ref, 12, 9))
+    own_rows = pl.ds(pl.multiple_of(me * depth, depth), depth)
+
+    def local_copy(i):
+        ref, start, count = parts[i]
+        return pltpu.make_async_copy(
+            ref.at[0, :, :, columns(seg)],
+            w_ref.at[pl.ds(seg * taps + start, count), own_rows],
+            local_sem.at[i],
+        )
+
+    def remote(src, dst, sems, index, device):
+        return pltpu.make_async_remote_copy(
+            src_ref=src,
+            dst_ref=dst,
+            send_sem=sems.at[(0,) + index],
+            recv_sem=sems.at[(1,) + index],
+            device_id=device,
+            device_id_type=MESH,
+        )
+
+    def y_copy(i):
+        ref, start, count = parts[i]
+        return remote(
+            ref.at[0, :, :, columns(peer)],
+            w_ref.at[pl.ds(seg * taps + start, count), own_rows],
+            y_sems,
+            (i,),
+            (peer, me),
+        )
+
+    for i in range(3):
+        y_copy(i).start()
+        local_copy(i).start()
+
+    groups = (
+        (0, (0,), ((0, 5), (5, 4))),
+        (0, (1, 2), ((9, 6), (15, 6))),
+        (1, (0,), ((0, 5), (5, 4))),
+        (1, (1, 2), ((9, 6), (15, 6))),
+    )
+    streams = tuple((way, sub) for sub in range(2) for way in range(2))
+    mid = depth // 2
+
+    def slab(g, q, step):
+        section, _, subs = groups[g]
+        way, sub = streams[q]
+        start, count = subs[sub]
+        owner = frame_at(pos - step if way == 0 else pos + step)
+        rows = pl.ds(pl.multiple_of(owner * depth + way * mid, mid), mid)
+        return w_ref.at[pl.ds(section * taps + start, count), rows]
+
+    def ring(g, q, step):
+        ref = slab(g, q, step)
+        return remote(ref, ref, ring_sems, (g, q, step), (seg, right if streams[q][0] == 0 else left))
+
+    def paired(g, q, step):
+        ref = slab(g, q, step)
+        return remote(ref, ref, pair_sems, (g, q, step), (seg, other))
+
+    every = range(len(streams))
+
+    def begin(g):
+        section, needed, _ = groups[g]
+
+        @pl.when(seg == section)
+        def _():
+            for i in needed:
+                local_copy(i).wait()
+
+        @pl.when(seg != section)
+        def _():
+            for i in needed:
+                y_copy(i).wait_recv()
+
+        for q in every:
+            ring(g, q, 0).start()
+            paired(g, q, 0).start()
+
+    def advance(g, step):
+        for q in every:
+            ring(g, q, step - 1).wait_recv()
+
+            @pl.when(step < n - 1)
+            def _():
+                ring(g, q, step).start()
+
+            paired(g, q, step).start()
+
+    def complete(g):
+        @pl.loop(0, n)
+        def _(step):
+            for q in every:
+                paired(g, q, step).wait_recv()
+
+    def build(x, clip, value, where):
+        width = value.shape[1]
+        wide = value.astype(jnp.float32)
+        place = lax.broadcasted_iota(jnp.int32, (cells, width), 0) % side
+        shifted = (
+            jnp.where(place == 0, 0.0, pltpu.roll(wide, 1, 0)).astype(jnp.bfloat16),
+            value,
+            jnp.where(place == side - 1, 0.0, pltpu.roll(wide, cells - 1, 0)).astype(jnp.bfloat16),
+        )
+        for dx in range(3):
+            x[dx, clip, 1 : side + 1, :, where] = shifted[dx].reshape(side, side, width)
+
+    def spatial_sum(x, clip, base):
+        total = None
+        for dy in range(3):
+            for dx in range(3):
+                view = x[dx, clip, dy : dy + side].reshape(cells, lanes)
+                term = jnp.dot(
+                    view, w_ref[base + 3 * dy + dx], preferred_element_type=jnp.float32
+                )
+                total = term if total is None else total + term
+        return total
+
+    def silu(u):
+        return u / (1.0 + jnp.exp(-u))
+
+    def a_copy(s, clip):
+        return remote(a_send.at[s, clip], a_recv.at[s, clip], a_sems, (s, clip), (peer, me))
+
+    def e_copy(clip):
+        return remote(e_mine.at[clip], e_recv.at[clip], e_sems, (clip,), (peer, me))
+
+    def t_copy(s, way, clip):
+        target = after if way == 0 else before
+        return remote(
+            t_send.at[s, way, clip], t_recv.at[s, way, clip], t_sems, (s, way, clip), (seg, target)
+        )
+
+    def first_conv(s, clip):
+        total = spatial_sum(xe, clip, s * taps)
+        a_send[s, clip] = silu(total).astype(jnp.bfloat16)
+        a_copy(s, clip).start()
+
+    def take_active(s, clip):
+        a_copy(s, clip).wait_recv()
+        build(xa, clip, a_send[s, clip], columns(seg))
+        build(xa, clip, a_recv[s, clip], columns(peer))
+
+    sends_on = (me < frames - 1, me > 0)
+    takes_on = (me > 0, me < frames - 1)
+
+    def mixed(s, clip, k):
+        view = xa[1, clip, 1 : side + 1].reshape(cells, lanes)
+        return jnp.dot(view, w_ref[s * taps + 9 + k], preferred_element_type=jnp.float32)
+
+    def send_terms(s, clip):
+        for way, k in ((0, 0), (1, 2)):
+            t_send[s, way, clip] = mixed(s, clip, k).astype(jnp.bfloat16)
+
+            @pl.when(sends_on[way])
+            def _():
+                t_copy(s, way, clip).start()
+
+    def second_conv(s, clip):
+        acc_ref[clip] = spatial_sum(xa, clip, s * taps + 12) + mixed(s, clip, 1)
+
+    def finished(s, clip):
+        for way in range(2):
+
+            @pl.when(takes_on[way])
+            def _():
+                t_copy(s, way, clip).wait_recv()
+                acc_ref[clip] = acc_ref[clip] + t_recv[s, way, clip].astype(jnp.float32)
+
+        return silu(acc_ref[clip])
+
+    def end_first(clip):
+        own = noisy_ref[clip, 0, :, :, columns(seg)].reshape(cells, half).astype(jnp.float32)
+        out = (own + finished(0, clip)).astype(jnp.bfloat16)
+        e_mine[clip] = ((out.astype(jnp.float32) + own) * skip_scale).astype(jnp.bfloat16)
+        e_copy(clip).start()
+
+    def take_entering(clip):
+        e_copy(clip).wait_recv()
+        build(xe, clip, e_mine[clip], columns(seg))
+        build(xe, clip, e_recv[clip], columns(peer))
+
+    def end_second(clip):
+        out = (e_mine[clip].astype(jnp.float32) + finished(1, clip)).astype(jnp.bfloat16)
+        o_full[clip] = out.reshape(side, side, half)
+        o_send(clip).start()
+
+    def o_send(clip):
+        slab_rows = side // 2
+        return remote(
+            o_full.at[clip, pl.ds(peer * slab_rows, slab_rows)],
+            o_take.at[clip],
+            o_sems,
+            (clip,),
+            (peer, me),
+        )
+
+    def staged(steps, plan):
+        for offset, work in plan:
+
+            @pl.when((steps >= offset) & (steps < offset + clips))
+            def _():
+                work(steps - offset)
+
+    def overlap(g, plan):
+        last = max([n] + [offset + clips for offset, _ in plan])
+
+        @pl.loop(1, last)
+        def _(step):
+            @pl.when(step < n)
+            def _():
+                advance(g, step)
+
+            if g + 1 < len(groups):
+
+                @pl.when(step == n - 2)
+                def _():
+                    begin(g + 1)
+
+            staged(step, plan)
+
+        complete(g)
+
+    begin(0)
+    edge = jnp.zeros((side, lanes), jnp.bfloat16)
+    for x in (xe, xa):
+        for dx in range(3):
+
+            @pl.loop(0, clips)
+            def _(clip):
+                x[dx, clip, 0] = edge
+                x[dx, clip, side + 1] = edge
+
+    overlap(0, ((1, lambda clip: build(xe, clip, noisy_ref[clip, 0].reshape(cells, lanes), slice(None))),))
+    overlap(1, ((1, lambda clip: first_conv(0, clip)), (4, lambda clip: take_active(0, clip))))
+
+    def both(s):
+        def work(clip):
+            send_terms(s, clip)
+            second_conv(s, clip)
+
+        return work
+
+    overlap(2, ((1, both(0)), (4, end_first)))
+    overlap(
+        3,
+        (
+            (1, take_entering),
+            (2, lambda clip: first_conv(1, clip)),
+            (4, lambda clip: take_active(1, clip)),
+        ),
+    )
+
+    @pl.loop(0, clips)
+    def _(clip):
+        send_terms(1, clip)
+
+    @pl.loop(0, clips)
+    def _(clip):
+        second_conv(1, clip)
+        end_second(clip)
+
+    slab_rows = side // 2
+
+    @pl.loop(0, clips)
+    def _(clip):
+        out_ref[clip, 0, :, :, columns(seg)] = o_full[clip, pl.ds(seg * slab_rows, slab_rows)]
+        o_send(clip).wait_recv()
+        out_ref[clip, 0, :, :, columns(peer)] = o_take[clip]
+        o_send(clip).wait_send()
+        e_copy(clip).wait_send()
+        for s in range(2):
+            a_copy(s, clip).wait_send()
+            for way in range(2):
+
+                @pl.when(sends_on[way])
+                def _():
+                    t_copy(s, way, clip).wait_send()
+
+    for i in range(3):
+        y_copy(i).wait_send()
+
+    @pl.loop(0, n)
+    def _(step):
+        for g in range(len(groups)):
+            for q in every:
+                paired(g, q, step).wait_send()
+
+                @pl.when(step < n - 1)
+                def _():
+                    ring(g, q, step).wait_send()
+
+
+def on_device(noisy_clips, conv_first, conv_second, temporal):
+    sections = lax.axis_size("segment")
+    frames = lax.axis_size("frame")
+    clips, frame_local, side, _, lanes = noisy_clips.shape
+    half = lanes // 2
+    cells = side * side
+    if sections != 2 or half % 128 or frames % 4 or frames < 8 or frame_local != 1 or side % 16:
+        return pipelined(noisy_clips, conv_first, conv_second, temporal)
+    n = frames // 2
+    dma = pltpu.SemaphoreType.DMA
+    vmem = pl.BlockSpec(memory_space=pltpu.VMEM)
+    kind = jnp.bfloat16
+    return pl.pallas_call(
+        functools.partial(fused_kernel, frames),
+        out_shape=jax.ShapeDtypeStruct((clips, 1, side // 2, side, lanes), kind),
+        in_specs=[vmem] * 4,
+        out_specs=vmem,
+        scratch_shapes=[
+            pltpu.VMEM((42, lanes, half), kind),
+            pltpu.VMEM((3, clips, side + 2, side, lanes), kind),
+            pltpu.VMEM((3, clips, side + 2, side, lanes), kind),
+            pltpu.VMEM((2, clips, cells, half), kind),
+            pltpu.VMEM((2, clips, cells, half), kind),
+            pltpu.VMEM((2, 2, clips, cells, half), kind),
+            pltpu.VMEM((2, 2, clips, cells, half), kind),
+            pltpu.VMEM((clips, cells, half), kind),
+            pltpu.VMEM((clips, cells, half), kind),
+            pltpu.VMEM((clips, cells, half), jnp.float32),
+            pltpu.VMEM((clips, side, side, half), kind),
+            pltpu.VMEM((clips, side // 2, side, half), kind),
+            dma((3,)),
+            dma((2, 3)),
+            dma((2, 4, 4, n)),
+            dma((2, 4, 4, n)),
+            dma((2, 2, clips)),
+            dma((2, 2, 2, clips)),
+            dma((2, clips)),
+            dma((2, clips)),
+        ],
+        compiler_params=pltpu.CompilerParams(
+            collective_id=0, has_side_effects=True, vmem_limit_bytes=58 * 1024 * 1024
+        ),
+    )(noisy_clips, conv_first, conv_second, temporal)
+
+
 def solution(mesh):
     in_specs = (
         P(None, "frame", None, None, None),

time: 430 us -> 129 us (0.30)
  waiting for transfers between devices: 266 us -> 0 us
  Pallas kernels: 0 us -> 127 us
  starting transfers between devices: 62.6 us -> 0 us
  matrix products: 50 us -> 0 us
  other arithmetic: 22 us -> 0 us
  between operations: 13.2 us -> 0.01 us
  local copies, waits for them, and re-layouts: 8.95 us -> 1.87 us
  loops' own time: 4.65 us -> 0 us
    all_gather x3 -> x0, waiting for transfers between devices: 148 us -> none  [the longest x1 54 us: on_device(): lax.all_gather(conv_first, 'frame', axis=2, tiled=True)]
    pallas_call x0 -> x1, Pallas kernels: none -> 127 us  [on_device(): pl.pallas_call(functools.partial(fused_kernel, frames), out_shape=jax.Sha...]
    ppermute x20 -> x0, starting transfers between devices: 62.5 us -> none  [the longest x5 27 us: extended_2(): lax.ppermute(tail, axis, [(i, (i + 1) % count) for i in range(ends)])]
    ppermute x20 -> x0, waiting for transfers between devices: 57.8 us -> none  [the longest x10 30.8 us: passed_along(): return lax.ppermute(shard, axis, pairs)]
    psum x1 -> x0, waiting for transfers between devices: 57.6 us -> none  [broadcast(): return lax.psum(jnp.where(mine, shard, jnp.zeros_like(shard)), axis)]
    dot_general x84 -> x0, matrix products: 50 us -> none  [the longest x72 39.3 us: spatial(): jnp.dot(window, kernel[3 * row_shift + col_shift], preferred_element_type...]
    select_n x11 -> x0, other arithmetic: 17.4 us -> none  [the longest x5 9.77 us: tick_step(): section_in = jnp.where(is_up, joined, entering)]
    dynamic_slice x6 -> x0, local copies, waits for them, and re-layouts: 5.22 us -> none  [the longest x5 3.36 us: on_device(): lax.scan(tick_step, (prev_out, side_store, out_store), jnp.arange(tick_co...]
  transfers between devices with their start and end apart: 24 -> 0, of which waited for: 21 -> 0; matrix products, arithmetic and copies ran while one was open for 1% -> 0% of each run, Pallas kernels for 0% -> 0%
where the time goes in v2:
time: 129 us
  Pallas kernels  127 us (98%)
  local copies, waits for them, and re-layouts  1.87 us (1%)
    pallas_call x1, Pallas kernels, on_device(): pl.pallas_call(functools.partial(fused_kernel, frames), out_shape=jax.Sha...  127 us

profile of v2, /device:TPU:2, one launch (start us, length us, event | category | flops | bytes accessed | tf_op | source)
XLA Modules:
  0.0 129.3 jit_solution(10467367897229434925)
XLA Ops:
  0.0 127.4 %shard_map.46 = bf16[4,1,8,16,512]{4,3,2,1,0:T(8,128)(2,1)} custom-call(bf16[4,1,16,16,512]{4,3,2,1,0:T(8,128)(2,1)} %noisy_ref.1, bf16[1,9,32,512]{3,2,1,0:T(8,128)(2,1)} %first_ref.1, bf16[1,9,32,512]{3,2,1,0:T(8,128)(2,1)} %second_ref.1, bf16[1,3,32,512]{3,2,1,0:T(8,128)(2,1)} %time_ref.1), custom_call_target="tpu_custom_call" | custom-call | tf_op jit(solution)/shard_map/pallas_call | solution.py:498
  127.4 1.9 %copy.6 = bf16[4,1,8,16,512]{4,3,2,1,0:T(8,128)(2,1)} copy(bf16[4,1,8,16,512]{4,3,2,1,0:T(8,128)(2,1)} %shard_map.46) | data formatting | bytes 1048576

commit v3 on v2

--- a/solution.py
+++ b/solution.py
@@ -394,26 +394,6 @@
             def _():
                 work(steps - offset)
 
-    def overlap(g, plan):
-        last = max([n] + [offset + clips for offset, _ in plan])
-
-        @pl.loop(1, last)
-        def _(step):
-            @pl.when(step < n)
-            def _():
-                advance(g, step)
-
-            if g + 1 < len(groups):
-
-                @pl.when(step == n - 2)
-                def _():
-                    begin(g + 1)
-
-            staged(step, plan)
-
-        complete(g)
-
-    begin(0)
     edge = jnp.zeros((side, lanes), jnp.bfloat16)
     for x in (xe, xa):
         for dx in range(3):
@@ -423,9 +403,6 @@
                 x[dx, clip, 0] = edge
                 x[dx, clip, side + 1] = edge
 
-    overlap(0, ((1, lambda clip: build(xe, clip, noisy_ref[clip, 0].reshape(cells, lanes), slice(None))),))
-    overlap(1, ((1, lambda clip: first_conv(0, clip)), (4, lambda clip: take_active(0, clip))))
-
     def both(s):
         def work(clip):
             send_terms(s, clip)
@@ -433,15 +410,39 @@
 
         return work
 
-    overlap(2, ((1, both(0)), (4, end_first)))
-    overlap(
-        3,
-        (
-            (1, take_entering),
-            (2, lambda clip: first_conv(1, clip)),
-            (4, lambda clip: take_active(1, clip)),
-        ),
+    skew = n // 2 - 1
+    ready = [g * skew + n for g in range(len(groups))]
+    start_terms = max(ready[1], ready[0] + 4)
+    start_next = max(ready[2], start_terms + 5)
+    plan = (
+        (0, lambda clip: build(xe, clip, noisy_ref[clip, 0].reshape(cells, lanes), slice(None))),
+        (ready[0], lambda clip: first_conv(0, clip)),
+        (start_terms - 1, lambda clip: take_active(0, clip)),
+        (start_terms, both(0)),
+        (start_terms + 2, end_first),
+        (start_next - 1, take_entering),
+        (start_next, lambda clip: first_conv(1, clip)),
+        (start_next + 3, lambda clip: take_active(1, clip)),
     )
+    last = max([ready[-1] + 1] + [offset + clips for offset, _ in plan])
+
+    @pl.loop(0, last)
+    def _(step):
+        for g in range(len(groups)):
+
+            @pl.when((step > g * skew) & (step < ready[g]))
+            def _():
+                advance(g, step - g * skew)
+
+            @pl.when(step == g * skew)
+            def _():
+                begin(g)
+
+            @pl.when(step == ready[g])
+            def _():
+                complete(g)
+
+        staged(step, plan)
 
     @pl.loop(0, clips)
     def _(clip):

time: 129 us -> 119 us (0.922)
  the two profiles are of different devices: /device:TPU:2 before, /device:TPU:22 now
where the time goes in v3:
time: 119 us
  Pallas kernels  117 us (98%)
  local copies, waits for them, and re-layouts  1.87 us (2%)
    pallas_call x1, Pallas kernels, on_device(): pl.pallas_call(functools.partial(fused_kernel, frames), out_shape=jax.Sha...  117 us

profile of v3, /device:TPU:22, one launch (start us, length us, event | category | flops | bytes accessed | tf_op | source)
XLA Modules:
  0.0 119.0 jit_solution(16885489603237898504)
XLA Ops:
  0.0 117.1 %shard_map.46 = bf16[4,1,8,16,512]{4,3,2,1,0:T(8,128)(2,1)} custom-call(bf16[4,1,16,16,512]{4,3,2,1,0:T(8,128)(2,1)} %noisy_ref.1, bf16[1,9,32,512]{3,2,1,0:T(8,128)(2,1)} %first_ref.1, bf16[1,9,32,512]{3,2,1,0:T(8,128)(2,1)} %second_ref.1, bf16[1,3,32,512]{3,2,1,0:T(8,128)(2,1)} %time_ref.1), custom_call_target="tpu_custom_call" | custom-call | tf_op jit(solution)/shard_map/pallas_call | solution.py:499
  117.1 1.9 %copy.6 = bf16[4,1,8,16,512]{4,3,2,1,0:T(8,128)(2,1)} copy(bf16[4,1,8,16,512]{4,3,2,1,0:T(8,128)(2,1)} %shard_map.46) | data formatting | bytes 1048576
